TPU v7x, 32 devices: a whole 2x2x4 slice. The times are simulated.
32 devices in a mesh: parts: 2 (over y), blk: 4 (over z), grp: 4 (over x, core).
Axes of the slice: x: 2, y: 2, z: 4, core: 2. Of those that a mesh axis runs over, the one named last changes fastest.
Arguments:
- factors: float32 [64, 4096], P(None, ('parts', 'blk', 'grp')), parts along dimension 1, may hold values from -1 to 1
- tangent: float32 [64, 4096], P(None, ('parts', 'blk', 'grp')), parts along dimension 1, may hold values from -15 to 15
- counts: int32 [4096, 2048], P(('parts', 'blk', 'grp')), parts along dimension 0, may hold values from 0 to 4, as said below
Outputs:
- hess_vec: float32 [64, 4096], P(None, ('parts', 'blk', 'grp')), parts along dimension 1
- residual: float32 [64, 4096], P(None, ('parts', 'blk', 'grp')), parts along dimension 1
- inner: float32 [4], P('parts'), parts along dimension 0
There are 2 independent parts, one for each index of `parts`. A program takes and returns all parts, laid end to end along the dimension named above; each array names one. Nothing has to cross between parts.
Inputs may be any that keep to these rules, and one draw needn't show every extreme that they name: counts is symmetric.
All inputs are finite; a program needn't handle non-finite values.
Results may differ from a plain program's by a relative error of at most 0.0003.
Values sent between devices are 32-bit elements; how exact they have to be, the bound alone decides.
A program may use at most 128 MiB of HBM per device.

v0:
```python
import jax
import jax.numpy as jnp
from jax import lax
from jax.sharding import PartitionSpec as P


def local(factors, tangent, counts):
    rows = counts.shape[0]
    nodes = counts.shape[1]
    scale = 1.0 / jnp.sqrt(jnp.float32(nodes))
    highest = lax.Precision.HIGHEST
    contract = (((0,), (0,)), ((), ()))
    right = (((1,), (1,)), ((), ()))
    row_start = (lax.axis_index("blk") * lax.axis_size("grp") + lax.axis_index("grp")) * rows
    row_ids = row_start + jnp.arange(rows, dtype=jnp.int32)[:, None]
    group_u, group_v = (
        lax.all_gather(factors, "grp", axis=1, tiled=True),
        lax.all_gather(tangent, "grp", axis=1, tiled=True),
    )
    piece_u = lax.all_gather(group_u, "blk", axis=1, tiled=True)
    piece_v = lax.all_gather(group_v, "blk", axis=1, tiled=True)
    width = piece_u.shape[1]
    eta = lax.dot_general(factors, piece_u, contract, precision=highest)
    deta = lax.dot_general(factors, piece_v, contract, precision=highest) + lax.dot_general(
        tangent, piece_u, contract, precision=highest
    )
    col_ids = jnp.arange(width, dtype=jnp.int32)[None, :]
    keep = row_ids != col_ids
    rate = jnp.where(keep, jnp.exp(eta), jnp.float32(0.0))
    weight = rate * deta
    tile_counts = counts.astype(jnp.float32)
    slack = jnp.where(keep, tile_counts - rate, jnp.float32(0.0))
    hess_acc = lax.dot_general(piece_u, weight, right, precision=highest)
    resid_acc = lax.dot_general(piece_u, slack - weight, right, precision=highest)
    hess_acc, resid_acc = (hess_acc, resid_acc)
    hess_vec = hess_acc * scale
    residual = resid_acc * scale
    sum_sq, sum_curv = lax.psum(
        (jnp.sum(residual * residual), jnp.sum(tangent * hess_vec)), ("blk", "grp")
    )
    inner = jnp.stack([sum_sq, sum_curv])
    return (hess_vec, residual, inner)


def solution(mesh):
    return jax.shard_map(
        local,
        mesh=mesh,
        in_specs=(
            P(None, ("parts", "blk", "grp")),
            P(None, ("parts", "blk", "grp")),
            P(("parts", "blk", "grp"), None),
        ),
        out_specs=(P(None, ("parts", "blk", "grp")), P(None, ("parts", "blk", "grp")), P("parts")),
        check_vma=False,
    )
```

profile of v0, /device:TPU:0, one launch (start us, length us, event | category | flops | bytes accessed | tf_op | source)
XLA Modules:
  0.0 85.9 jit_solution(17943244656120877728)
XLA Ops:
  0.6 0.0 copy-start.1
  0.7 6.7 %all_gather.12 = f32[64,512]{1,0:T(8,128)S(1)} all-gather(f32[64,128]{1,0:T(8,128)} %param.3), channel_id=1, replica_groups=mesh['parts'=2,'blk'=4,'grp'=4] {'grp'}, dimensions={1}, use_global_device_ids=true | all-gather | bytes 163840 | tf_op jit(solution)/shard_map/all_gather | solution.py:17
  7.4 0.0 copy-done.1
  7.4 5.6 %all_gather.14 = f32[64,512]{1,0:T(8,128)S(1)} all-gather(f32[64,128]{1,0:T(8,128)S(1)} %copy-done.1), channel_id=1, replica_groups=mesh['parts'=2,'blk'=4,'grp'=4] {'grp'}, dimensions={1}, use_global_device_ids=true | all-gather | bytes 163840 | tf_op jit(solution)/shard_map/all_gather | solution.py:18
  12.9 16.6 %all_gather.13 = f32[64,2048]{1,0:T(8,128)S(1)} all-gather(f32[64,512]{1,0:T(8,128)S(1)} %all_gather.12), channel_id=1, replica_groups=mesh['parts'=2,'blk'=4,'grp'=4] {'blk'}, dimensions={1}, use_global_device_ids=true | all-gather | bytes 655360 | tf_op jit(solution)/shard_map/all_gather | solution.py:20
  29.5 0.0 copy-start.2
  29.5 16.0 %all_gather.15 = f32[64,2048]{1,0:T(8,128)S(1)} all-gather(f32[64,512]{1,0:T(8,128)S(1)} %all_gather.14), channel_id=1, replica_groups=mesh['parts'=2,'blk'=4,'grp'=4] {'blk'}, dimensions={1}, use_global_device_ids=true | all-gather | bytes 655360 | tf_op jit(solution)/shard_map/all_gather | solution.py:21
  45.5 0.0 copy-done.2
  45.5 1.0 %fusion.11 = f32[128,2048]{1,0:T(8,128)S(1)} fusion(f32[64,128]{1,0:T(8,128)S(1)} %copy-done.2, f32[64,2048]{1,0:T(8,128)S(1)} %all_gather.15), kind=kOutput, calls=%fused_computation.20 | convolution fusion | flops 201326592 | bytes 1605632 | tf_op jit(solution)/shard_map/dot_general | solution.py:24
  46.6 1.1 %fusion.1 = f32[128,2048]{1,0:T(8,128)S(1)} fusion(f32[64,128]{1,0:T(8,128)S(1)} %copy-done.2, f32[64,2048]{1,0:T(8,128)S(1)} %all_gather.13, s32[128]{0:T(128)S(1)} %iota_add_fusion), kind=kOutput, calls=%fused_computation.3 | convolution fusion | flops 201850880 | bytes 1606144 | tf_op jit(solution)/shard_map/dot_general | solution.py:23
  47.7 0.0 copy-start
  47.7 1.1 %fusion = f32[128,2048]{1,0:T(8,128)S(1)} fusion(f32[128,2048]{1,0:T(8,128)S(1)} %fusion.1, f32[128,2048]{1,0:T(8,128)S(1)} %fusion.11, f32[64,128]{1,0:T(8,128)S(1)} %copy-done.1, f32[64,2048]{1,0:T(8,128)S(1)} %all_gather.13), kind=kOutput, calls=%fused_computation.1 | convolution fusion | flops 201850880 | bytes 3702784 | tf_op jit(solution)/shard_map/dot_general | solution.py:24
  48.8 0.2 copy-done
  48.9 2.7 %multiply_reduce_fusion.1 = (f32[]{:T(128)}, f32[64,128]{1,0:T(8,128)}) fusion(f32[64,2048]{1,0:T(8,128)S(1)} %all_gather.13, f32[128,2048]{1,0:T(8,128)S(1)} %fusion, f32[128,2048]{1,0:T(8,128)S(1)} %fusion.1, s32[128,2048]{1,0:T(8,128)S(1)} %copy-done, s32[128]{0:T(128)S(1)} %iota_add_fusion), kind=kOutput, calls=%fused_computation.16 | convolution fusion | flops 202661888 | bytes 3703300 | tf_op jit(solution)/shard_map/dot_general | solution.py:34
  51.6 2.4 %multiply_reduce_fusion = (f32[]{:T(128)}, f32[64,128]{1,0:T(8,128)}) fusion(f32[64,128]{1,0:T(8,128)S(1)} %copy-done.1, f32[128,2048]{1,0:T(8,128)S(1)} %fusion, f32[64,2048]{1,0:T(8,128)S(1)} %all_gather.13), kind=kOutput, calls=%fused_computation.15 | convolution fusion | flops 201351168 | bytes 1638404 | tf_op jit(solution)/shard_map/dot_general | solution.py:33
  54.0 30.1 %all-reduce = (f32[1]{0:T(128)}, f32[1]{0:T(128)}) all-reduce(f32[1]{0:T(128)} %bitcast.3, f32[1]{0:T(128)} %bitcast.2), channel_id=1, replica_groups=mesh['parts'=2,'blk'=4,'grp'=4] {'blk','grp'}, use_global_device_ids=true, to_apply=%region_3.4 | all-reduce | flops 2 | bytes 16 | tf_op jit(solution)/shard_map/psum | solution.py:38
  84.2 1.8 %pad_maximum_fusion = f32[2]{0:T(128)} fusion(f32[1]{0:T(128)} %get-tuple-element.3, f32[1]{0:T(128)} %get-tuple-element.4), kind=kLoop, calls=%fused_computation.17 | loop fusion | flops 2 | bytes 16 | tf_op jit(solution)/shard_map/stack | solution.py:41
  (1 shorter events, 0.0 us)
Async XLA Ops:
  0.6 6.7 %copy-start.1 = (f32[64,128]{1,0:T(8,128)S(1)}, f32[64,128]{1,0:T(8,128)}, u32[]{:S(2)}) copy-start(f32[64,128]{1,0:T(8,128)} %param.4) | copy-start | bytes 98308
  29.5 16.0 %copy-start.2 = (f32[64,128]{1,0:T(8,128)S(1)}, f32[64,128]{1,0:T(8,128)}, u32[]{:S(2)}) copy-start(f32[64,128]{1,0:T(8,128)} %param.3) | copy-start | bytes 98308
  47.7 1.2 %copy-start = (s32[128,2048]{1,0:T(8,128)S(1)}, s32[128,2048]{1,0:T(8,128)}, u32[]{:S(2)}) copy-start(s32[128,2048]{1,0:T(8,128)} %param.5) | copy-start | bytes 3145732
where the time goes:
time: 86.3 us; the launch traced here: 85.9 us
  blocking collectives  75 us (87%)
  matrix products  8.3 us (10%)
  other arithmetic  1.78 us (2%)
    psum x1, blocking collectives, local(): lax.psum((jnp.sum(residual * residual), jnp.sum(tangent * hess_vec)), ('b...  30.1 us
    all_gather x1, blocking collectives, local(): piece_u = lax.all_gather(group_u, 'blk', axis=1, tiled=True)  16.6 us
    all_gather x1, blocking collectives, local(): piece_v = lax.all_gather(group_v, 'blk', axis=1, tiled=True)  16 us
    all_gather x1, blocking collectives, local(): lax.all_gather(factors, 'grp', axis=1, tiled=True)  6.69 us
    all_gather x1, blocking collectives, local(): lax.all_gather(tangent, 'grp', axis=1, tiled=True)  5.58 us
    dot_general x1, matrix products, local(): lax.dot_general(piece_u, slack - weight, right, precision=highest)  2.69 us
    dot_general x1, matrix products, local(): hess_acc = lax.dot_general(piece_u, weight, right, precision=highest)  2.41 us
    another operation x1, other arithmetic, local(): inner = jnp.stack([sum_sq, sum_curv])  1.78 us

commit v1 on v0

--- a/solution.py
+++ b/solution.py
@@ -36,7 +36,7 @@
     hess_vec = hess_acc * scale
     residual = resid_acc * scale
     sum_sq, sum_curv = lax.psum(
-        (jnp.sum(residual * residual), jnp.sum(tangent * hess_vec)), ("blk", "grp")
+        lax.psum((jnp.sum(residual * residual), jnp.sum(tangent * hess_vec)), "grp"), "blk"
     )
     inner = jnp.stack([sum_sq, sum_curv])
     return (hess_vec, residual, inner)

time: 86.3 us -> 74.4 us (0.86)
  blocking collectives: 75 us -> 63.2 us
    psum x1 -> x2, blocking collectives: 30.1 us -> 18.3 us  [the longest x1 12 us: local(): lax.psum(lax.psum((jnp.sum(residual * residual), jnp.sum(tangent * hess_v...]
where the time goes in v1:
time: 74.4 us; the launch traced here: 74 us
  blocking collectives  63.2 us (85%)
  matrix products  8.22 us (11%)
  other arithmetic  1.78 us (2%)
    all_gather x1, blocking collectives, local(): piece_u = lax.all_gather(group_u, 'blk', axis=1, tiled=True)  16.6 us
    all_gather x1, blocking collectives, local(): piece_v = lax.all_gather(group_v, 'blk', axis=1, tiled=True)  16 us
    psum x1, blocking collectives, local(): lax.psum(lax.psum((jnp.sum(residual * residual), jnp.sum(tangent * hess_v...  12 us
    all_gather x1, blocking collectives, local(): lax.all_gather(factors, 'grp', axis=1, tiled=True)  6.69 us
    psum x1, blocking collectives, local(): lax.psum((jnp.sum(residual * residual), jnp.sum(tangent * hess_vec)), 'grp')  6.35 us
    all_gather x1, blocking collectives, local(): lax.all_gather(tangent, 'grp', axis=1, tiled=True)  5.58 us
    dot_general x1, matrix products, local(): lax.dot_general(piece_u, slack - weight, right, precision=highest)  2.6 us
    dot_general x1, matrix products, local(): hess_acc = lax.dot_general(piece_u, weight, right, precision=highest)  2.41 us

profile of v1, /device:TPU:0, one launch (start us, length us, event | category | flops | bytes accessed | tf_op | source)
XLA Modules:
  0.0 74.0 jit_solution(2162573603261192260)
XLA Ops:
  0.6 0.0 copy-start.1
  0.7 6.7 %all_gather.12 = f32[64,512]{1,0:T(8,128)S(1)} all-gather(f32[64,128]{1,0:T(8,128)} %param.3), channel_id=1, replica_groups=mesh['parts'=2,'blk'=4,'grp'=4] {'grp'}, dimensions={1}, use_global_device_ids=true | all-gather | bytes 163840 | tf_op jit(solution)/shard_map/all_gather | solution.py:17
  7.4 0.0 copy-done.1
  7.4 5.6 %all_gather.14 = f32[64,512]{1,0:T(8,128)S(1)} all-gather(f32[64,128]{1,0:T(8,128)S(1)} %copy-done.1), channel_id=1, replica_groups=mesh['parts'=2,'blk'=4,'grp'=4] {'grp'}, dimensions={1}, use_global_device_ids=true | all-gather | bytes 163840 | tf_op jit(solution)/shard_map/all_gather | solution.py:18
  12.9 16.6 %all_gather.13 = f32[64,2048]{1,0:T(8,128)S(1)} all-gather(f32[64,512]{1,0:T(8,128)S(1)} %all_gather.12), channel_id=1, replica_groups=mesh['parts'=2,'blk'=4,'grp'=4] {'blk'}, dimensions={1}, use_global_device_ids=true | all-gather | bytes 655360 | tf_op jit(solution)/shard_map/all_gather | solution.py:20
  29.5 0.0 copy-start.2
  29.5 16.0 %all_gather.15 = f32[64,2048]{1,0:T(8,128)S(1)} all-gather(f32[64,512]{1,0:T(8,128)S(1)} %all_gather.14), channel_id=1, replica_groups=mesh['parts'=2,'blk'=4,'grp'=4] {'blk'}, dimensions={1}, use_global_device_ids=true | all-gather | bytes 655360 | tf_op jit(solution)/shard_map/all_gather | solution.py:21
  45.5 0.0 copy-done.2
  45.5 1.0 %fusion.11 = f32[128,2048]{1,0:T(8,128)S(1)} fusion(f32[64,128]{1,0:T(8,128)S(1)} %copy-done.2, f32[64,2048]{1,0:T(8,128)S(1)} %all_gather.15), kind=kOutput, calls=%fused_computation.20 | convolution fusion | flops 201326592 | bytes 1605632 | tf_op jit(solution)/shard_map/dot_general | solution.py:24
  46.6 1.1 %fusion.1 = f32[128,2048]{1,0:T(8,128)S(1)} fusion(f32[64,128]{1,0:T(8,128)S(1)} %copy-done.2, f32[64,2048]{1,0:T(8,128)S(1)} %all_gather.13, s32[128]{0:T(128)S(1)} %iota_add_fusion), kind=kOutput, calls=%fused_computation.3 | convolution fusion | flops 201850880 | bytes 1606144 | tf_op jit(solution)/shard_map/dot_general | solution.py:23
  47.7 0.0 copy-start
  47.7 1.1 %fusion = f32[128,2048]{1,0:T(8,128)S(1)} fusion(f32[128,2048]{1,0:T(8,128)S(1)} %fusion.1, f32[128,2048]{1,0:T(8,128)S(1)} %fusion.11, f32[64,128]{1,0:T(8,128)S(1)} %copy-done.1, f32[64,2048]{1,0:T(8,128)S(1)} %all_gather.13), kind=kOutput, calls=%fused_computation.1 | convolution fusion | flops 201850880 | bytes 3702784 | tf_op jit(solution)/shard_map/dot_general | solution.py:24
  48.8 0.2 copy-done
  48.9 2.6 %multiply_reduce_fusion.1 = (f32[]{:T(128)}, f32[64,128]{1,0:T(8,128)}) fusion(f32[64,2048]{1,0:T(8,128)S(1)} %all_gather.13, f32[128,2048]{1,0:T(8,128)S(1)} %fusion, f32[128,2048]{1,0:T(8,128)S(1)} %fusion.1, s32[128,2048]{1,0:T(8,128)S(1)} %copy-done, s32[128]{0:T(128)S(1)} %iota_add_fusion), kind=kOutput, calls=%fused_computation.16 | convolution fusion | flops 202661888 | bytes 3703300 | tf_op jit(solution)/shard_map/dot_general | solution.py:34
  51.5 2.4 %multiply_reduce_fusion = (f32[]{:T(128)}, f32[64,128]{1,0:T(8,128)}) fusion(f32[64,128]{1,0:T(8,128)S(1)} %copy-done.1, f32[128,2048]{1,0:T(8,128)S(1)} %fusion, f32[64,2048]{1,0:T(8,128)S(1)} %all_gather.13), kind=kOutput, calls=%fused_computation.15 | convolution fusion | flops 201351168 | bytes 1638404 | tf_op jit(solution)/shard_map/dot_general | solution.py:33
  53.9 6.3 %all-reduce = (f32[]{:T(128)}, f32[]{:T(128)}) all-reduce(f32[]{:T(128)} %get-tuple-element.7, f32[]{:T(128)} %get-tuple-element.9), channel_id=1, replica_groups=mesh['parts'=2,'blk'=4,'grp'=4] {'grp'}, use_global_device_ids=true, to_apply=%region_4.5 | all-reduce | flops 2 | bytes 16 | tf_op jit(solution)/shard_map/psum | solution.py:39
  60.3 12.0 %all-reduce.1 = (f32[1]{0:T(128)}, f32[1]{0:T(128)}) all-reduce(f32[1]{0:T(128)} %bitcast.3, f32[1]{0:T(128)} %bitcast.2), channel_id=1, replica_groups=mesh['parts'=2,'blk'=4,'grp'=4] {'blk'}, use_global_device_ids=true, to_apply=%region_5.6 | all-reduce | flops 2 | bytes 16 | tf_op jit(solution)/shard_map/psum | solution.py:38
  72.3 1.8 %pad_maximum_fusion = f32[2]{0:T(128)} fusion(f32[1]{0:T(128)} %get-tuple-element.5, f32[1]{0:T(128)} %get-tuple-element.6), kind=kLoop, calls=%fused_computation.17 | loop fusion | flops 2 | bytes 16 | tf_op jit(solution)/shard_map/stack | solution.py:41
  (1 shorter events, 0.0 us)
Async XLA Ops:
  0.6 6.7 %copy-start.1 = (f32[64,128]{1,0:T(8,128)S(1)}, f32[64,128]{1,0:T(8,128)}, u32[]{:S(2)}) copy-start(f32[64,128]{1,0:T(8,128)} %param.4) | copy-start | bytes 98308
  29.5 16.0 %copy-start.2 = (f32[64,128]{1,0:T(8,128)S(1)}, f32[64,128]{1,0:T(8,128)}, u32[]{:S(2)}) copy-start(f32[64,128]{1,0:T(8,128)} %param.3) | copy-start | bytes 98308
  47.7 1.2 %copy-start = (s32[128,2048]{1,0:T(8,128)S(1)}, s32[128,2048]{1,0:T(8,128)}, u32[]{:S(2)}) copy-start(s32[128,2048]{1,0:T(8,128)} %param.5) | copy-start | bytes 3145732
